TPU v7x, 512 devices: a whole 4x4x16 slice. The times are simulated.
512 devices in a mesh: ctx: 16 (over y, x_hi, core), fsdp: 32 (over z, x_lo).
Axes of the slice: x: 4 (x_hi: 2, x_lo: 2; x = x_hi * 2 + x_lo), y: 4, z: 16, core: 2. Of those that a mesh axis runs over, the one named last changes fastest.
Arguments:
- query_states: bfloat16 [32, 2048, 2048], P('fsdp', 'ctx'), may hold values from -12 to 12
- key_states: bfloat16 [32, 2048, 512], P('fsdp', 'ctx'), may hold values from -24 to 24
- value_states: bfloat16 [32, 2048, 512], P('fsdp', 'ctx'), may hold values from -170 to 170
- doc_ids: int32 [32, 2048], P('fsdp', 'ctx'), may hold values from 0 to 7, never falling along the last dimension, each value on 1 to 1536 neighbouring positions
- routes: int32 [32, 2048, 2], P('fsdp', 'ctx'), may hold values from 0 to 7, as said below
- route_weight: bfloat16 [32, 2048, 2], P('fsdp', 'ctx'), may hold values from 0.19921875 to 1
- cotangent: bfloat16 [32, 2048, 2048], P('fsdp', 'ctx'), may hold values from -6 to 6
- gate_weight: bfloat16 [2048, 7168], P('fsdp', 'ctx'), may hold values from -0.125 to 0.125
- up_weight: bfloat16 [2048, 7168], P('fsdp', 'ctx'), may hold values from -0.125 to 0.125
- down_weight: bfloat16 [7168, 2048], P('ctx', 'fsdp'), may hold values from -0.0625 to 0.0625
Outputs:
- attn_out: bfloat16 [32, 2048, 2048], P('fsdp', 'ctx')
- d_input: bfloat16 [32, 2048, 2048], P('fsdp', 'ctx')
Inputs may be any that keep to these rules, and one draw needn't show every extreme that they name: `routes`: each token names 2 different experts. Of the 128 tokens of one block of a sequence, at most 8 name expert 0; in some sequence every block has exactly 8 such tokens.
All inputs are finite; a program needn't handle non-finite values.
Results may differ from a plain program's by a relative error of at most 0.02.
Values may be sent and summed in bfloat16 or wider, within the bound.
No kernel may reach another device: no remote copies, remote signals or barrier semaphores. Data moves between devices by JAX's collectives and lax.ppermute only.
A program may use at most 64 MiB of HBM per device.

v0:
```python
import jax
import jax.numpy as jnp
from jax import lax
from jax.sharding import PartitionSpec as P

HEADS = 16
KV_HEADS = 4
HEAD_DIM = 128
CAP = 8
epsilon = 1e-05
far_below = -1e30


def from_behind(shard, axis, by):
    length = lax.axis_size(axis)
    return lax.ppermute(shard, axis, [(i, (i + by) % length) for i in range(length)])


def on_device(
    query_states,
    key_states,
    value_states,
    doc_ids,
    routes,
    route_weight,
    cotangent,
    gate_weight,
    up_weight,
    down_weight,
):
    gate_panel, up_panel, down_panel = (
        lax.all_gather(gate_weight, "fsdp", axis=0, tiled=True),
        lax.all_gather(up_weight, "fsdp", axis=0, tiled=True),
        lax.all_gather(down_weight, "fsdp", axis=1, tiled=True),
    )
    every_doc = lax.all_gather(doc_ids, "ctx", axis=1, tiled=True)[0]
    cycle_size = lax.axis_size("ctx")
    position = lax.axis_index("ctx")
    tok_count = query_states.shape[1]
    model_width = query_states.shape[2]
    group_size = HEADS // KV_HEADS
    scaling = HEAD_DIM ** (-0.5)
    query_heads = query_states[0].reshape(tok_count, KV_HEADS, group_size, HEAD_DIM)
    query_docs = lax.dynamic_slice_in_dim(every_doc, position * tok_count, tok_count)

    def attend_block(running, key_block, source):
        key_heads = key_block[0].reshape(tok_count, KV_HEADS, HEAD_DIM)
        value_heads = key_block[1].reshape(tok_count, KV_HEADS, HEAD_DIM)
        key_docs = lax.dynamic_slice_in_dim(every_doc, source * tok_count, tok_count)
        allowed = key_docs[None, :] == query_docs[:, None]
        row_max, row_total, weighted = running
        scores = (
            jnp.einsum("igrd,jgd->grij", query_heads, key_heads, preferred_element_type=jnp.float32)
            * scaling
        )
        masked = jnp.where(allowed, scores, far_below)
        new_max = jnp.maximum(row_max, jnp.max(masked, axis=-1))
        unscaled = jnp.where(allowed, jnp.exp(masked - new_max[..., None]), 0.0)
        factor = jnp.exp(row_max - new_max)
        probabilities = unscaled.astype(jnp.bfloat16)
        weighted = weighted * factor[..., None] + jnp.einsum(
            "grij,jgd->grid", probabilities, value_heads, preferred_element_type=jnp.float32
        )
        return (new_max, row_total * factor + jnp.sum(unscaled, axis=-1), weighted)

    own_block = (key_states[0], value_states[0])
    start_state = (
        jnp.full((KV_HEADS, group_size, tok_count), far_below, jnp.float32),
        jnp.zeros((KV_HEADS, group_size, tok_count), jnp.float32),
        jnp.zeros((KV_HEADS, group_size, tok_count, HEAD_DIM), jnp.float32),
    )
    running = attend_block(start_state, own_block, position)

    def cycle_step(step_index, loop_state):
        running_now, key_block = loop_state
        key_block = from_behind((key_block[0], key_block[1]), "ctx", 1)
        return (
            attend_block(running_now, key_block, (position - step_index) % cycle_size),
            key_block,
        )

    running, last_block = lax.fori_loop(1, cycle_size, cycle_step, (running, own_block))
    row_max, row_total, weighted = running
    mixed = weighted / row_total[..., None]
    attn_out = (
        jnp.transpose(mixed, (2, 0, 1, 3)).reshape(tok_count, model_width).astype(jnp.bfloat16)
    )
    as_float = attn_out.astype(jnp.float32)
    inverse = lax.rsqrt(jnp.mean(as_float * as_float, axis=-1, keepdims=True) + epsilon)
    scaled = as_float * inverse
    normed = scaled.astype(jnp.bfloat16)
    chosen = routes[0] == 0
    routed = jnp.any(chosen, axis=-1)
    weight = jnp.sum(jnp.where(chosen, route_weight[0].astype(jnp.float32), 0.0), axis=-1)
    slot_index = jnp.cumsum(routed.astype(jnp.int32)) - 1
    selector = (slot_index[None, :] == jnp.arange(CAP, dtype=jnp.int32)[:, None]) & routed[None, :]
    selector_half = selector.astype(jnp.bfloat16)
    selector_float = selector.astype(jnp.float32)
    slot_x = jnp.dot(selector_half, normed, preferred_element_type=jnp.float32).astype(jnp.bfloat16)
    slot_dy = jnp.dot(selector_half, cotangent[0], preferred_element_type=jnp.float32).astype(
        jnp.bfloat16
    )
    slot_w = jnp.dot(selector_float, weight, precision=lax.Precision.HIGHEST).astype(jnp.bfloat16)
    rows_x, rows_dy, rows_w = (
        lax.all_gather(slot_x, "ctx", axis=0, tiled=True),
        lax.all_gather(slot_dy, "ctx", axis=0, tiled=True),
        lax.all_gather(slot_w, "ctx", axis=0, tiled=True),
    )
    contract_last = (((1,), (1,)), ((), ()))
    gate_proj = jnp.dot(rows_x, gate_panel, preferred_element_type=jnp.float32)
    up_proj = jnp.dot(rows_x, up_panel, preferred_element_type=jnp.float32)
    back_grad = lax.dot_general(
        rows_dy, down_panel, contract_last, preferred_element_type=jnp.float32
    )
    back_grad = back_grad * rows_w.astype(jnp.float32)[:, None]
    sigmoid_gate = jax.nn.sigmoid(gate_proj)
    grad_gate = (
        back_grad * up_proj * sigmoid_gate * (1.0 + gate_proj * (1.0 - sigmoid_gate))
    ).astype(jnp.bfloat16)
    grad_up = (back_grad * gate_proj * sigmoid_gate).astype(jnp.bfloat16)
    result = lax.dot_general(
        grad_gate, gate_panel, contract_last, preferred_element_type=jnp.float32
    )
    d_slots = lax.psum_scatter(
        (
            result
            + lax.dot_general(grad_up, up_panel, contract_last, preferred_element_type=jnp.float32)
        ).astype(jnp.bfloat16),
        "ctx",
        scatter_dimension=0,
        tiled=True,
    ).astype(jnp.float32)
    d_norm = jnp.dot(selector_float.T, d_slots, precision=lax.Precision.HIGHEST)
    d_input = inverse * (d_norm - scaled * jnp.mean(d_norm * scaled, axis=-1, keepdims=True))
    return (attn_out[None], d_input.astype(jnp.bfloat16)[None])


def solution(mesh):
    return jax.shard_map(
        on_device,
        mesh=mesh,
        in_specs=(
            P("fsdp", "ctx", None),
            P("fsdp", "ctx", None),
            P("fsdp", "ctx", None),
            P("fsdp", "ctx"),
            P("fsdp", "ctx", None),
            P("fsdp", "ctx", None),
            P("fsdp", "ctx", None),
            P("fsdp", "ctx"),
            P("fsdp", "ctx"),
            P("ctx", "fsdp"),
        ),
        out_specs=(P("fsdp", "ctx", None), P("fsdp", "ctx", None)),
        check_vma=False,
    )
```

profile of v0, /device:TPU:32, one launch (start us, length us, event | category | flops | bytes accessed | tf_op | source)
XLA Modules:
  0.0 520.8 jit_solution(569136732008379769)
XLA Ops:
  13.4 24.6 %all_gather.21 = s32[1,2048]{1,0:T(1,128)S(1)} all-gather(s32[1,128]{1,0:T(1,128)} %param.15), channel_id=1, replica_groups=mesh['ctx'=16,'fsdp'=32] {'ctx'}, dimensions={1}, use_global_device_ids=true | all-gather | bytes 8704 | tf_op jit(solution)/shard_map/all_gather | solution.py:36
  40.8 206.7 %while.23 = (s32[]{:T(128)}, f32[4,4,128]{2,1,0:T(4,128)S(1)}, f32[4,4,128]{2,1,0:T(4,128)S(1)}, f32[4,4,128,128]{3,2,1,0:T(8,128)S(1)}, bf16[128,512]{0,1:T(8,1...) while((s32[]{:T(128)}, f32[4,4,128]{2,1,0:T(4,128)S(1)}, ...), condition=%wide.region_5.6_spmd, body=%wide.region_2.5_spmd.sunk | while | flops 137121808 | bytes 7801232 | solution.py:82
  40.9 2.3 collective-permute-start
  43.1 1.9 collective-permute-start.1
  45.2 5.8 %collective-permute-done = bf16[128,512]{0,1:T(8,128)(2,1)S(1)} collective-permute-done((bf16[128,512]{0,1:T(8,128)(2,1)S(1)}, bf16[128,512]{0,1:T(8,128)(2,1)S(1)}, u32[]{:S(2)}, u32[]{:S(2)}) %collective-permute-start) | collective-permute-done | bytes 131104 | tf_op jit(solution)/shard_map/while/body/eval_jaxpr/ppermute | solution.py:16
  51.6 2.8 collective-permute-done.1
  55.2 1.9 collective-permute-start
  57.1 1.9 collective-permute-start.1
  59.2 7.0 %collective-permute-done = bf16[128,512]{0,1:T(8,128)(2,1)S(1)} collective-permute-done((bf16[128,512]{0,1:T(8,128)(2,1)S(1)}, bf16[128,512]{0,1:T(8,128)(2,1)S(1)}, u32[]{:S(2)}, u32[]{:S(2)}) %collective-permute-start) | collective-permute-done | bytes 131104 | tf_op jit(solution)/shard_map/while/body/eval_jaxpr/ppermute | solution.py:16
  66.9 1.8 collective-permute-done.1
  69.4 1.9 collective-permute-start
  71.3 1.9 collective-permute-start.1
  73.5 7.0 %collective-permute-done = bf16[128,512]{0,1:T(8,128)(2,1)S(1)} collective-permute-done((bf16[128,512]{0,1:T(8,128)(2,1)S(1)}, bf16[128,512]{0,1:T(8,128)(2,1)S(1)}, u32[]{:S(2)}, u32[]{:S(2)}) %collective-permute-start) | collective-permute-done | bytes 131104 | tf_op jit(solution)/shard_map/while/body/eval_jaxpr/ppermute | solution.py:16
  83.4 1.9 collective-permute-start
  85.3 1.9 collective-permute-start.1
  87.4 7.3 %collective-permute-done = bf16[128,512]{0,1:T(8,128)(2,1)S(1)} collective-permute-done((bf16[128,512]{0,1:T(8,128)(2,1)S(1)}, bf16[128,512]{0,1:T(8,128)(2,1)S(1)}, u32[]{:S(2)}, u32[]{:S(2)}) %collective-permute-start) | collective-permute-done | bytes 131104 | tf_op jit(solution)/shard_map/while/body/eval_jaxpr/ppermute | solution.py:16
  97.4 1.9 collective-permute-start
  99.3 1.9 collective-permute-start.1
  101.4 7.2 %collective-permute-done = bf16[128,512]{0,1:T(8,128)(2,1)S(1)} collective-permute-done((bf16[128,512]{0,1:T(8,128)(2,1)S(1)}, bf16[128,512]{0,1:T(8,128)(2,1)S(1)}, u32[]{:S(2)}, u32[]{:S(2)}) %collective-permute-start) | collective-permute-done | bytes 131104 | tf_op jit(solution)/shard_map/while/body/eval_jaxpr/ppermute | solution.py:16
  109.2 1.8 collective-permute-done.1
  111.7 1.9 collective-permute-start
  113.7 1.9 collective-permute-start.1
  115.8 6.4 %collective-permute-done = bf16[128,512]{0,1:T(8,128)(2,1)S(1)} collective-permute-done((bf16[128,512]{0,1:T(8,128)(2,1)S(1)}, bf16[128,512]{0,1:T(8,128)(2,1)S(1)}, u32[]{:S(2)}, u32[]{:S(2)}) %collective-permute-start) | collective-permute-done | bytes 131104 | tf_op jit(solution)/shard_map/while/body/eval_jaxpr/ppermute | solution.py:16
  122.8 2.1 collective-permute-done.1
  125.6 1.9 collective-permute-start
  127.5 1.9 collective-permute-start.1
  129.7 6.4 %collective-permute-done = bf16[128,512]{0,1:T(8,128)(2,1)S(1)} collective-permute-done((bf16[128,512]{0,1:T(8,128)(2,1)S(1)}, bf16[128,512]{0,1:T(8,128)(2,1)S(1)}, u32[]{:S(2)}, u32[]{:S(2)}) %collective-permute-start) | collective-permute-done | bytes 131104 | tf_op jit(solution)/shard_map/while/body/eval_jaxpr/ppermute | solution.py:16
  138.4 1.9 collective-permute-start
  140.4 1.9 collective-permute-start.1
  142.5 6.2 %collective-permute-done = bf16[128,512]{0,1:T(8,128)(2,1)S(1)} collective-permute-done((bf16[128,512]{0,1:T(8,128)(2,1)S(1)}, bf16[128,512]{0,1:T(8,128)(2,1)S(1)}, u32[]{:S(2)}, u32[]{:S(2)}) %collective-permute-start) | collective-permute-done | bytes 131104 | tf_op jit(solution)/shard_map/while/body/eval_jaxpr/ppermute | solution.py:16
  151.1 1.9 collective-permute-start
  153.0 1.9 collective-permute-start.1
  155.1 5.8 %collective-permute-done = bf16[128,512]{0,1:T(8,128)(2,1)S(1)} collective-permute-done((bf16[128,512]{0,1:T(8,128)(2,1)S(1)}, bf16[128,512]{0,1:T(8,128)(2,1)S(1)}, u32[]{:S(2)}, u32[]{:S(2)}) %collective-permute-start) | collective-permute-done | bytes 131104 | tf_op jit(solution)/shard_map/while/body/eval_jaxpr/ppermute | solution.py:16
  163.6 1.9 collective-permute-start
  165.6 1.9 collective-permute-start.1
  167.7 6.2 %collective-permute-done = bf16[128,512]{0,1:T(8,128)(2,1)S(1)} collective-permute-done((bf16[128,512]{0,1:T(8,128)(2,1)S(1)}, bf16[128,512]{0,1:T(8,128)(2,1)S(1)}, u32[]{:S(2)}, u32[]{:S(2)}) %collective-permute-start) | collective-permute-done | bytes 131104 | tf_op jit(solution)/shard_map/while/body/eval_jaxpr/ppermute | solution.py:16
  174.5 2.3 collective-permute-done.1
  177.6 1.9 collective-permute-start
  179.5 1.9 collective-permute-start.1
  181.6 7.0 %collective-permute-done = bf16[128,512]{0,1:T(8,128)(2,1)S(1)} collective-permute-done((bf16[128,512]{0,1:T(8,128)(2,1)S(1)}, bf16[128,512]{0,1:T(8,128)(2,1)S(1)}, u32[]{:S(2)}, u32[]{:S(2)}) %collective-permute-start) | collective-permute-done | bytes 131104 | tf_op jit(solution)/shard_map/while/body/eval_jaxpr/ppermute | solution.py:16
  191.6 1.9 collective-permute-start
  193.5 1.9 collective-permute-start.1
  195.6 7.1 %collective-permute-done = bf16[128,512]{0,1:T(8,128)(2,1)S(1)} collective-permute-done((bf16[128,512]{0,1:T(8,128)(2,1)S(1)}, bf16[128,512]{0,1:T(8,128)(2,1)S(1)}, u32[]{:S(2)}, u32[]{:S(2)}) %collective-permute-start) | collective-permute-done | bytes 131104 | tf_op jit(solution)/shard_map/while/body/eval_jaxpr/ppermute | solution.py:16
  205.8 1.9 collective-permute-start
  207.7 1.9 collective-permute-start.1
  209.9 6.8 %collective-permute-done = bf16[128,512]{0,1:T(8,128)(2,1)S(1)} collective-permute-done((bf16[128,512]{0,1:T(8,128)(2,1)S(1)}, bf16[128,512]{0,1:T(8,128)(2,1)S(1)}, u32[]{:S(2)}, u32[]{:S(2)}) %collective-permute-start) | collective-permute-done | bytes 131104 | tf_op jit(solution)/shard_map/while/body/eval_jaxpr/ppermute | solution.py:16
  217.3 1.8 collective-permute-done.1
  219.9 1.9 collective-permute-start
  221.8 1.9 collective-permute-start.1
  223.9 6.3 %collective-permute-done = bf16[128,512]{0,1:T(8,128)(2,1)S(1)} collective-permute-done((bf16[128,512]{0,1:T(8,128)(2,1)S(1)}, bf16[128,512]{0,1:T(8,128)(2,1)S(1)}, u32[]{:S(2)}, u32[]{:S(2)}) %collective-permute-start) | collective-permute-done | bytes 131104 | tf_op jit(solution)/shard_map/while/body/eval_jaxpr/ppermute | solution.py:16
  230.8 2.1 collective-permute-done.1
  233.6 1.9 collective-permute-start
  235.6 1.9 collective-permute-start.1
  237.7 6.3 %collective-permute-done = bf16[128,512]{0,1:T(8,128)(2,1)S(1)} collective-permute-done((bf16[128,512]{0,1:T(8,128)(2,1)S(1)}, bf16[128,512]{0,1:T(8,128)(2,1)S(1)}, u32[]{:S(2)}, u32[]{:S(2)}) %collective-permute-start) | collective-permute-done | bytes 131104 | tf_op jit(solution)/shard_map/while/body/eval_jaxpr/ppermute | solution.py:16
  244.6 2.3 collective-permute-done.1
  254.2 33.2 %all-reduce = bf16[128]{0:T(256)(128)(2,1)S(1)} all-reduce(bf16[128]{0:T(256)(128)(2,1)S(1)} %dynamic-update-slice), channel_id=1, replica_groups=mesh['ctx'=16,'fsdp'=32] {'ctx'}, use_global_device_ids=true, to_apply=%add | all-reduce | flops 128 | bytes 512
  287.9 22.7 %all_gather.25 = bf16[128,2048]{1,0:T(8,128)(2,1)S(1)} all-gather(bf16[8,2048]{1,0:T(8,128)(2,1)S(1)} %convolution_convert_fusion), channel_id=1, replica_groups=mesh['ctx'=16,'fsdp'=32] {'ctx'}, dimensions={0}, use_global_device_ids=true | all-gather | bytes 557056 | tf_op jit(solution)/shard_map/all_gather | solution.py:105
  310.6 27.7 %all_gather.22 = bf16[128,2048]{1,0:T(8,128)(2,1)S(1)} all-gather(bf16[8,2048]{1,0:T(8,128)(2,1)S(1)} %convolution_convert_fusion.1), channel_id=1, replica_groups=mesh['ctx'=16,'fsdp'=32] {'ctx'}, dimensions={0}, use_global_device_ids=true | all-gather | bytes 557056 | tf_op jit(solution)/shard_map/all_gather | solution.py:106
  338.3 3.2 fusion.55
  341.5 2.5 convolution_multiply_fusion.3
  344.0 71.4 %all-gather.6.cloned.1.call-done = bf16[2048,448]{1,0:T(8,128)(2,1)} async-done(((bf16[64,448]{1,0:T(8,128)(2,1)}), bf16[2048,448]{1,0:T(8,128)(2,1)}) %all-gather.6.cloned.1.call-update) | async-done | bytes 1835024 | tf_op jit(solution)/shard_map/all_gather | solution.py:33
  415.4 5.5 %fusion.15 = f32[128,2048]{1,0:T(8,128)} fusion(bf16[2048,448]{1,0:T(8,128)(2,1)} %all-gather.8.cloned.1.call-done, f32[128,448]{0,1:T(8,128)S(1)} %convolution_multiply_fusion.3, bf16[128,2048]{1,0:T(8,128)(2,1)S(1)} %all_gather.25, bf16[2048,448]{1,0:T(8,128)(2,1)} %all-gather.6.cloned.1.call-done, f32[128,448]{0,1:T(8,128)} %fusion.55), kind=kOutput, calls=%fused_computation.27 | convolution fusion | flops 470335488 | bytes 5701632 | tf_op jit(solution)/shard_map/dot_general | solution.py:121
  420.8 3.5 fusion.9
  426.0 86.1 %reduce-scatter.2.cloned.1.call-done = bf16[8,2048]{1,0:T(8,128)(2,1)} async-done(((bf16[128,2048]{1,0:T(8,128)(2,1)}), bf16[8,2048]{1,0:T(8,128)(2,1)}) %reduce-scatter.2.cloned.1.call-update) | async-done | bytes 32784 | tf_op jit(solution)/shard_map/reduce_scatter | solution.py:124
  (211 shorter events, 50.6 us)
Async XLA Ops:
  7.2 280.3 %copy-start = (bf16[1,128,2048]{2,1,0:T(8,128)(2,1)S(1)}, bf16[1,128,2048]{2,1,0:T(8,128)(2,1)}, u32[]{:S(2)}) copy-start(bf16[1,128,2048]{2,1,0:T(8,128)(2,1)} %param.18) | copy-start | bytes 1572868
  7.2 331.1 %all-gather.8.cloned.1.call-start = ((), (), s32[]{:S(2)}) async-start(), calls=%async_computation.3 | async-start | bytes 2162688 | tf_op jit(solution)/shard_map/all_gather | solution.py:32
  7.9 333.6 %all-gather.4.cloned.1.call-start = ((), (), s32[]{:S(2)}) async-start(), calls=%async_computation.1 | async-start | bytes 2162688 | tf_op jit(solution)/shard_map/all_gather | solution.py:34
  8.7 406.7 %all-gather.6.cloned.1.call-start = ((), (), s32[]{:S(2)}) async-start(), calls=%async_computation.2 | async-start | bytes 2162688 | tf_op jit(solution)/shard_map/all_gather | solution.py:33
  9.4 502.6 %reduce-scatter.2.cloned.1.call-start = ((), (), s32[]{:S(2)}) async-start(), calls=%async_computation.4 | async-start | bytes 557056 | tf_op jit(solution)/shard_map/reduce_scatter | solution.py:124
  40.9 10.2 %collective-permute-start = (bf16[128,512]{0,1:T(8,128)(2,1)S(1)}, bf16[128,512]{0,1:T(8,128)(2,1)S(1)}, u32[]{:S(2)}, u32[]{:S(2)}) collective-permute-start(bf16[128,512]{0,1:T(8,128)(2,1)S(1)} %get-tuple-element.383), channel_id=1, source_target_pairs={{0,32},{32,64},{64,96},{96,128},{128,160},{160,192},{192,224},{224... | collective-permute-start | bytes 393224 | tf_op jit(solution)/shard_map/while/body/eval_jaxpr/ppermute | solution.py:16
  43.1 11.3 %collective-permute-start.1 = (bf16[128,512]{0,1:T(8,128)(2,1)S(1)}, bf16[128,512]{0,1:T(8,128)(2,1)S(1)}, u32[]{:S(2)}, u32[]{:S(2)}) collective-permute-start(bf16[128,512]{0,1:T(8,128)(2,1)S(1)} %get-tuple-element.384), channel_id=1, source_target_pairs={{0,32},{32,64},{64,96},{96,128},{128,160},{160,192},{192,224},{224... | collective-permute-start | bytes 393224 | tf_op jit(solution)/shard_map/while/body/eval_jaxpr/ppermute | solution.py:16
  55.2 11.1 %collective-permute-start = (bf16[128,512]{0,1:T(8,128)(2,1)S(1)}, bf16[128,512]{0,1:T(8,128)(2,1)S(1)}, u32[]{:S(2)}, u32[]{:S(2)}) collective-permute-start(bf16[128,512]{0,1:T(8,128)(2,1)S(1)} %get-tuple-element.383), channel_id=1, source_target_pairs={{0,32},{32,64},{64,96},{96,128},{128,160},{160,192},{192,224},{224... | collective-permute-start | bytes 393224 | tf_op jit(solution)/shard_map/while/body/eval_jaxpr/ppermute | solution.py:16
  57.1 11.6 %collective-permute-start.1 = (bf16[128,512]{0,1:T(8,128)(2,1)S(1)}, bf16[128,512]{0,1:T(8,128)(2,1)S(1)}, u32[]{:S(2)}, u32[]{:S(2)}) collective-permute-start(bf16[128,512]{0,1:T(8,128)(2,1)S(1)} %get-tuple-element.384), channel_id=1, source_target_pairs={{0,32},{32,64},{64,96},{96,128},{128,160},{160,192},{192,224},{224... | collective-permute-start | bytes 393224 | tf_op jit(solution)/shard_map/while/body/eval_jaxpr/ppermute | solution.py:16
  69.4 11.0 %collective-permute-start = (bf16[128,512]{0,1:T(8,128)(2,1)S(1)}, bf16[128,512]{0,1:T(8,128)(2,1)S(1)}, u32[]{:S(2)}, u32[]{:S(2)}) collective-permute-start(bf16[128,512]{0,1:T(8,128)(2,1)S(1)} %get-tuple-element.383), channel_id=1, source_target_pairs={{0,32},{32,64},{64,96},{96,128},{128,160},{160,192},{192,224},{224... | collective-permute-start | bytes 393224 | tf_op jit(solution)/shard_map/while/body/eval_jaxpr/ppermute | solution.py:16
  71.3 11.3 %collective-permute-start.1 = (bf16[128,512]{0,1:T(8,128)(2,1)S(1)}, bf16[128,512]{0,1:T(8,128)(2,1)S(1)}, u32[]{:S(2)}, u32[]{:S(2)}) collective-permute-start(bf16[128,512]{0,1:T(8,128)(2,1)S(1)} %get-tuple-element.384), channel_id=1, source_target_pairs={{0,32},{32,64},{64,96},{96,128},{128,160},{160,192},{192,224},{224... | collective-permute-start | bytes 393224 | tf_op jit(solution)/shard_map/while/body/eval_jaxpr/ppermute | solution.py:16
  83.4 11.4 %collective-permute-start = (bf16[128,512]{0,1:T(8,128)(2,1)S(1)}, bf16[128,512]{0,1:T(8,128)(2,1)S(1)}, u32[]{:S(2)}, u32[]{:S(2)}) collective-permute-start(bf16[128,512]{0,1:T(8,128)(2,1)S(1)} %get-tuple-element.383), channel_id=1, source_target_pairs={{0,32},{32,64},{64,96},{96,128},{128,160},{160,192},{192,224},{224... | collective-permute-start | bytes 393224 | tf_op jit(solution)/shard_map/while/body/eval_jaxpr/ppermute | solution.py:16
  85.3 11.3 %collective-permute-start.1 = (bf16[128,512]{0,1:T(8,128)(2,1)S(1)}, bf16[128,512]{0,1:T(8,128)(2,1)S(1)}, u32[]{:S(2)}, u32[]{:S(2)}) collective-permute-start(bf16[128,512]{0,1:T(8,128)(2,1)S(1)} %get-tuple-element.384), channel_id=1, source_target_pairs={{0,32},{32,64},{64,96},{96,128},{128,160},{160,192},{192,224},{224... | collective-permute-start | bytes 393224 | tf_op jit(solution)/shard_map/while/body/eval_jaxpr/ppermute | solution.py:16
  97.4 11.2 %collective-permute-start = (bf16[128,512]{0,1:T(8,128)(2,1)S(1)}, bf16[128,512]{0,1:T(8,128)(2,1)S(1)}, u32[]{:S(2)}, u32[]{:S(2)}) collective-permute-start(bf16[128,512]{0,1:T(8,128)(2,1)S(1)} %get-tuple-element.383), channel_id=1, source_target_pairs={{0,32},{32,64},{64,96},{96,128},{128,160},{160,192},{192,224},{224... | collective-permute-start | bytes 393224 | tf_op jit(solution)/shard_map/while/body/eval_jaxpr/ppermute | solution.py:16
  99.3 11.7 %collective-permute-start.1 = (bf16[128,512]{0,1:T(8,128)(2,1)S(1)}, bf16[128,512]{0,1:T(8,128)(2,1)S(1)}, u32[]{:S(2)}, u32[]{:S(2)}) collective-permute-start(bf16[128,512]{0,1:T(8,128)(2,1)S(1)} %get-tuple-element.384), channel_id=1, source_target_pairs={{0,32},{32,64},{64,96},{96,128},{128,160},{160,192},{192,224},{224... | collective-permute-start | bytes 393224 | tf_op jit(solution)/shard_map/while/body/eval_jaxpr/ppermute | solution.py:16
  111.7 10.4 %collective-permute-start = (bf16[128,512]{0,1:T(8,128)(2,1)S(1)}, bf16[128,512]{0,1:T(8,128)(2,1)S(1)}, u32[]{:S(2)}, u32[]{:S(2)}) collective-permute-start(bf16[128,512]{0,1:T(8,128)(2,1)S(1)} %get-tuple-element.383), channel_id=1, source_target_pairs={{0,32},{32,64},{64,96},{96,128},{128,160},{160,192},{192,224},{224... | collective-permute-start | bytes 393224 | tf_op jit(solution)/shard_map/while/body/eval_jaxpr/ppermute | solution.py:16
  113.7 11.2 %collective-permute-start.1 = (bf16[128,512]{0,1:T(8,128)(2,1)S(1)}, bf16[128,512]{0,1:T(8,128)(2,1)S(1)}, u32[]{:S(2)}, u32[]{:S(2)}) collective-permute-start(bf16[128,512]{0,1:T(8,128)(2,1)S(1)} %get-tuple-element.384), channel_id=1, source_target_pairs={{0,32},{32,64},{64,96},{96,128},{128,160},{160,192},{192,224},{224... | collective-permute-start | bytes 393224 | tf_op jit(solution)/shard_map/while/body/eval_jaxpr/ppermute | solution.py:16
  125.6 10.4 %collective-permute-start = (bf16[128,512]{0,1:T(8,128)(2,1)S(1)}, bf16[128,512]{0,1:T(8,128)(2,1)S(1)}, u32[]{:S(2)}, u32[]{:S(2)}) collective-permute-start(bf16[128,512]{0,1:T(8,128)(2,1)S(1)} %get-tuple-element.383), channel_id=1, source_target_pairs={{0,32},{32,64},{64,96},{96,128},{128,160},{160,192},{192,224},{224... | collective-permute-start | bytes 393224 | tf_op jit(solution)/shard_map/while/body/eval_jaxpr/ppermute | solution.py:16
  127.5 10.2 %collective-permute-start.1 = (bf16[128,512]{0,1:T(8,128)(2,1)S(1)}, bf16[128,512]{0,1:T(8,128)(2,1)S(1)}, u32[]{:S(2)}, u32[]{:S(2)}) collective-permute-start(bf16[128,512]{0,1:T(8,128)(2,1)S(1)} %get-tuple-element.384), channel_id=1, source_target_pairs={{0,32},{32,64},{64,96},{96,128},{128,160},{160,192},{192,224},{224... | collective-permute-start | bytes 393224 | tf_op jit(solution)/shard_map/while/body/eval_jaxpr/ppermute | solution.py:16
  138.4 10.3 %collective-permute-start = (bf16[128,512]{0,1:T(8,128)(2,1)S(1)}, bf16[128,512]{0,1:T(8,128)(2,1)S(1)}, u32[]{:S(2)}, u32[]{:S(2)}) collective-permute-start(bf16[128,512]{0,1:T(8,128)(2,1)S(1)} %get-tuple-element.383), channel_id=1, source_target_pairs={{0,32},{32,64},{64,96},{96,128},{128,160},{160,192},{192,224},{224... | collective-permute-start | bytes 393224 | tf_op jit(solution)/shard_map/while/body/eval_jaxpr/ppermute | solution.py:16
  140.4 10.0 %collective-permute-start.1 = (bf16[128,512]{0,1:T(8,128)(2,1)S(1)}, bf16[128,512]{0,1:T(8,128)(2,1)S(1)}, u32[]{:S(2)}, u32[]{:S(2)}) collective-permute-start(bf16[128,512]{0,1:T(8,128)(2,1)S(1)} %get-tuple-element.384), channel_id=1, source_target_pairs={{0,32},{32,64},{64,96},{96,128},{128,160},{160,192},{192,224},{224... | collective-permute-start | bytes 393224 | tf_op jit(solution)/shard_map/while/body/eval_jaxpr/ppermute | solution.py:16
  151.1 9.9 %collective-permute-start = (bf16[128,512]{0,1:T(8,128)(2,1)S(1)}, bf16[128,512]{0,1:T(8,128)(2,1)S(1)}, u32[]{:S(2)}, u32[]{:S(2)}) collective-permute-start(bf16[128,512]{0,1:T(8,128)(2,1)S(1)} %get-tuple-element.383), channel_id=1, source_target_pairs={{0,32},{32,64},{64,96},{96,128},{128,160},{160,192},{192,224},{224... | collective-permute-start | bytes 393224 | tf_op jit(solution)/shard_map/while/body/eval_jaxpr/ppermute | solution.py:16
  153.0 9.9 %collective-permute-start.1 = (bf16[128,512]{0,1:T(8,128)(2,1)S(1)}, bf16[128,512]{0,1:T(8,128)(2,1)S(1)}, u32[]{:S(2)}, u32[]{:S(2)}) collective-permute-start(bf16[128,512]{0,1:T(8,128)(2,1)S(1)} %get-tuple-element.384), channel_id=1, source_target_pairs={{0,32},{32,64},{64,96},{96,128},{128,160},{160,192},{192,224},{224... | collective-permute-start | bytes 393224 | tf_op jit(solution)/shard_map/while/body/eval_jaxpr/ppermute | solution.py:16
  163.6 10.3 %collective-permute-start = (bf16[128,512]{0,1:T(8,128)(2,1)S(1)}, bf16[128,512]{0,1:T(8,128)(2,1)S(1)}, u32[]{:S(2)}, u32[]{:S(2)}) collective-permute-start(bf16[128,512]{0,1:T(8,128)(2,1)S(1)} %get-tuple-element.383), channel_id=1, source_target_pairs={{0,32},{32,64},{64,96},{96,128},{128,160},{160,192},{192,224},{224... | collective-permute-start | bytes 393224 | tf_op jit(solution)/shard_map/while/body/eval_jaxpr/ppermute | solution.py:16
  165.6 11.3 %collective-permute-start.1 = (bf16[128,512]{0,1:T(8,128)(2,1)S(1)}, bf16[128,512]{0,1:T(8,128)(2,1)S(1)}, u32[]{:S(2)}, u32[]{:S(2)}) collective-permute-start(bf16[128,512]{0,1:T(8,128)(2,1)S(1)} %get-tuple-element.384), channel_id=1, source_target_pairs={{0,32},{32,64},{64,96},{96,128},{128,160},{160,192},{192,224},{224... | collective-permute-start | bytes 393224 | tf_op jit(solution)/shard_map/while/body/eval_jaxpr/ppermute | solution.py:16
  177.6 11.0 %collective-permute-start = (bf16[128,512]{0,1:T(8,128)(2,1)S(1)}, bf16[128,512]{0,1:T(8,128)(2,1)S(1)}, u32[]{:S(2)}, u32[]{:S(2)}) collective-permute-start(bf16[128,512]{0,1:T(8,128)(2,1)S(1)} %get-tuple-element.383), channel_id=1, source_target_pairs={{0,32},{32,64},{64,96},{96,128},{128,160},{160,192},{192,224},{224... | collective-permute-start | bytes 393224 | tf_op jit(solution)/shard_map/while/body/eval_jaxpr/ppermute | solution.py:16
  179.5 11.4 %collective-permute-start.1 = (bf16[128,512]{0,1:T(8,128)(2,1)S(1)}, bf16[128,512]{0,1:T(8,128)(2,1)S(1)}, u32[]{:S(2)}, u32[]{:S(2)}) collective-permute-start(bf16[128,512]{0,1:T(8,128)(2,1)S(1)} %get-tuple-element.384), channel_id=1, source_target_pairs={{0,32},{32,64},{64,96},{96,128},{128,160},{160,192},{192,224},{224... | collective-permute-start | bytes 393224 | tf_op jit(solution)/shard_map/while/body/eval_jaxpr/ppermute | solution.py:16
  191.6 11.1 %collective-permute-start = (bf16[128,512]{0,1:T(8,128)(2,1)S(1)}, bf16[128,512]{0,1:T(8,128)(2,1)S(1)}, u32[]{:S(2)}, u32[]{:S(2)}) collective-permute-start(bf16[128,512]{0,1:T(8,128)(2,1)S(1)} %get-tuple-element.383), channel_id=1, source_target_pairs={{0,32},{32,64},{64,96},{96,128},{128,160},{160,192},{192,224},{224... | collective-permute-start | bytes 393224 | tf_op jit(solution)/shard_map/while/body/eval_jaxpr/ppermute | solution.py:16
  193.5 11.6 %collective-permute-start.1 = (bf16[128,512]{0,1:T(8,128)(2,1)S(1)}, bf16[128,512]{0,1:T(8,128)(2,1)S(1)}, u32[]{:S(2)}, u32[]{:S(2)}) collective-permute-start(bf16[128,512]{0,1:T(8,128)(2,1)S(1)} %get-tuple-element.384), channel_id=1, source_target_pairs={{0,32},{32,64},{64,96},{96,128},{128,160},{160,192},{192,224},{224... | collective-permute-start | bytes 393224 | tf_op jit(solution)/shard_map/while/body/eval_jaxpr/ppermute | solution.py:16
  205.8 10.9 %collective-permute-start = (bf16[128,512]{0,1:T(8,128)(2,1)S(1)}, bf16[128,512]{0,1:T(8,128)(2,1)S(1)}, u32[]{:S(2)}, u32[]{:S(2)}) collective-permute-start(bf16[128,512]{0,1:T(8,128)(2,1)S(1)} %get-tuple-element.383), channel_id=1, source_target_pairs={{0,32},{32,64},{64,96},{96,128},{128,160},{160,192},{192,224},{224... | collective-permute-start | bytes 393224 | tf_op jit(solution)/shard_map/while/body/eval_jaxpr/ppermute | solution.py:16
  207.7 11.4 %collective-permute-start.1 = (bf16[128,512]{0,1:T(8,128)(2,1)S(1)}, bf16[128,512]{0,1:T(8,128)(2,1)S(1)}, u32[]{:S(2)}, u32[]{:S(2)}) collective-permute-start(bf16[128,512]{0,1:T(8,128)(2,1)S(1)} %get-tuple-element.384), channel_id=1, source_target_pairs={{0,32},{32,64},{64,96},{96,128},{128,160},{160,192},{192,224},{224... | collective-permute-start | bytes 393224 | tf_op jit(solution)/shard_map/while/body/eval_jaxpr/ppermute | solution.py:16
  219.9 10.3 %collective-permute-start = (bf16[128,512]{0,1:T(8,128)(2,1)S(1)}, bf16[128,512]{0,1:T(8,128)(2,1)S(1)}, u32[]{:S(2)}, u32[]{:S(2)}) collective-permute-start(bf16[128,512]{0,1:T(8,128)(2,1)S(1)} %get-tuple-element.383), channel_id=1, source_target_pairs={{0,32},{32,64},{64,96},{96,128},{128,160},{160,192},{192,224},{224... | collective-permute-start | bytes 393224 | tf_op jit(solution)/shard_map/while/body/eval_jaxpr/ppermute | solution.py:16
  221.8 11.1 %collective-permute-start.1 = (bf16[128,512]{0,1:T(8,128)(2,1)S(1)}, bf16[128,512]{0,1:T(8,128)(2,1)S(1)}, u32[]{:S(2)}, u32[]{:S(2)}) collective-permute-start(bf16[128,512]{0,1:T(8,128)(2,1)S(1)} %get-tuple-element.384), channel_id=1, source_target_pairs={{0,32},{32,64},{64,96},{96,128},{128,160},{160,192},{192,224},{224... | collective-permute-start | bytes 393224 | tf_op jit(solution)/shard_map/while/body/eval_jaxpr/ppermute | solution.py:16
  233.6 10.3 %collective-permute-start = (bf16[128,512]{0,1:T(8,128)(2,1)S(1)}, bf16[128,512]{0,1:T(8,128)(2,1)S(1)}, u32[]{:S(2)}, u32[]{:S(2)}) collective-permute-start(bf16[128,512]{0,1:T(8,128)(2,1)S(1)} %get-tuple-element.383), channel_id=1, source_target_pairs={{0,32},{32,64},{64,96},{96,128},{128,160},{160,192},{192,224},{224... | collective-permute-start | bytes 393224 | tf_op jit(solution)/shard_map/while/body/eval_jaxpr/ppermute | solution.py:16
  235.6 11.3 %collective-permute-start.1 = (bf16[128,512]{0,1:T(8,128)(2,1)S(1)}, bf16[128,512]{0,1:T(8,128)(2,1)S(1)}, u32[]{:S(2)}, u32[]{:S(2)}) collective-permute-start(bf16[128,512]{0,1:T(8,128)(2,1)S(1)} %get-tuple-element.384), channel_id=1, source_target_pairs={{0,32},{32,64},{64,96},{96,128},{128,160},{160,192},{192,224},{224... | collective-permute-start | bytes 393224 | tf_op jit(solution)/shard_map/while/body/eval_jaxpr/ppermute | solution.py:16
  248.1 3.4 copy-start.2
  248.1 5.6 %copy-start.3 = (bf16[1,128,2]{1,2,0:T(2,128)(2,1)S(1)}, bf16[1,128,2]{1,2,0:T(2,128)(2,1)}, u32[]{:S(2)}) copy-start(bf16[1,128,2]{1,2,0:T(2,128)(2,1)} %param.17) | copy-start | bytes 1540
  344.0 76.9 %copy-start.1 = (f32[128,448]{0,1:T(8,128)S(1)}, f32[128,448]{0,1:T(8,128)}, u32[]{:S(2)}) copy-start(f32[128,448]{0,1:T(8,128)} %fusion.55) | copy-start | bytes 688132
Sparse Core Ops, SparseCore 0:
  10.1 136.2 all-gather.7
  148.5 132.0 all-gather.3
  282.6 132.7 all-gather.5
  424.5 87.4 reduce-scatter.1
where the time goes:
time: 522 us; the launch traced here: 521 us
  waiting for transfers between devices  285 us (55%)
  blocking collectives  108 us (21%)
  starting transfers between devices  58.1 us (11%)
  matrix products  32.9 us (6%)
  between operations  14.6 us (3%)
  local copies, waits for them, and re-layouts  13.6 us (3%)
  other arithmetic  6.84 us (1%)
    ppermute x30, waiting for transfers between devices, from_behind(): lax.ppermute(shard, axis, [(i, (i + by) % length) for i in range(length)])  125 us
    reduce_scatter x1, waiting for transfers between devices, on_device(): lax.psum_scatter((result + lax.dot_general(grad_up, up_panel, contract_la...  86.1 us
    all_gather x1, waiting for transfers between devices, on_device(): lax.all_gather(up_weight, 'fsdp', axis=0, tiled=True)  71.4 us
    ppermute x30, starting transfers between devices, from_behind(): lax.ppermute(shard, axis, [(i, (i + by) % length) for i in range(length)])  57.9 us
    unnamed x1, blocking collectives  33.2 us
    all_gather x1, blocking collectives, on_device(): lax.all_gather(slot_dy, 'ctx', axis=0, tiled=True)  27.7 us
    all_gather x1, blocking collectives, on_device(): every_doc = lax.all_gather(doc_ids, 'ctx', axis=1, tiled=True)[0]  24.6 us
    all_gather x1, blocking collectives, on_device(): lax.all_gather(slot_x, 'ctx', axis=0, tiled=True)  22.7 us
  transfers between devices with their start and end apart: 34, of which 32 were waited for; matrix products, arithmetic and copies ran while one was open for 8% of the time, Pallas kernels for 0%

commit v1 on v0

--- a/solution.py
+++ b/solution.py
@@ -30,7 +30,12 @@
 ):
     gate_panel, up_panel, down_panel = (
         lax.all_gather(gate_weight, "fsdp", axis=0, tiled=True),
-        lax.all_gather(up_weight, "fsdp", axis=0, tiled=True),
+        jnp.concatenate(
+            lax.all_to_all(
+                jnp.stack([up_weight for _ in range(lax.axis_size("fsdp"))], 0), "fsdp", 0, 0
+            ),
+            0,
+        ),
         lax.all_gather(down_weight, "fsdp", axis=1, tiled=True),
     )
     every_doc = lax.all_gather(doc_ids, "ctx", axis=1, tiled=True)[0]

time: 522 us -> 461 us (0.88)
  waiting for transfers between devices: 285 us -> 214 us
  starting transfers between devices: 58.1 us -> 74.5 us
    all_gather x1 -> x0, waiting for transfers between devices: 71.4 us -> none  [on_device(): lax.all_gather(up_weight, 'fsdp', axis=0, tiled=True)]
    all_to_all x0 -> x1, starting transfers between devices: none -> 16.5 us  [on_device(): lax.all_to_all(jnp.stack([up_weight for _ in range(lax.axis_size('fsdp'))...]
    all_gather x1, blocking collectives: 27.7 us -> 21.6 us  [on_device(): lax.all_gather(slot_dy, 'ctx', axis=0, tiled=True)]
  transfers between devices with their start and end apart: 34 -> 34, of which waited for: 32 -> 31; matrix products, arithmetic and copies ran while one was open for 8% -> 9% of each run, Pallas kernels for 0% -> 0%
where the time goes in v1:
time: 461 us; the launch traced here: 460 us
  waiting for transfers between devices  214 us (46%)
  blocking collectives  104 us (23%)
  starting transfers between devices  74.5 us (16%)
  matrix products  32.9 us (7%)
  between operations  14.6 us (3%)
  local copies, waits for them, and re-layouts  11.4 us (2%)
  other arithmetic  6.84 us (1%)
    ppermute x30, waiting for transfers between devices, from_behind(): lax.ppermute(shard, axis, [(i, (i + by) % length) for i in range(length)])  130 us
    reduce_scatter x1, waiting for transfers between devices, on_device(): lax.psum_scatter((result + lax.dot_general(grad_up, up_panel, contract_la...  82.6 us
    ppermute x30, starting transfers between devices, from_behind(): lax.ppermute(shard, axis, [(i, (i + by) % length) for i in range(length)])  57.9 us
    unnamed x1, blocking collectives  33.4 us
    all_gather x1, blocking collectives, on_device(): lax.all_gather(slot_x, 'ctx', axis=0, tiled=True)  24.4 us
    all_gather x1, blocking collectives, on_device(): every_doc = lax.all_gather(doc_ids, 'ctx', axis=1, tiled=True)[0]  24.1 us
    all_gather x1, blocking collectives, on_device(): lax.all_gather(slot_dy, 'ctx', axis=0, tiled=True)  21.6 us
    all_to_all x1, starting transfers between devices, on_device(): lax.all_to_all(jnp.stack([up_weight for _ in range(lax.axis_size('fsdp'))...  16.5 us
  transfers between devices with their start and end apart: 34, of which 31 were waited for; matrix products, arithmetic and copies ran while one was open for 9% of the time, Pallas kernels for 0%

profile of v1, /device:TPU:32, one launch (start us, length us, event | category | flops | bytes accessed | tf_op | source)
XLA Modules:
  0.0 460.0 jit_solution(8201696028737586967)
XLA Ops:
  7.9 2.4 stack.2
  10.3 16.5 %all-to-all-start = ((bf16[32,64,448]{2,1,0:T(8,128)(2,1)}), bf16[32,64,448]{2,1,0:T(8,128)(2,1)}, u32[]{:S(2)}, u32[]{:S(2)}) async-start(bf16[32,64,448]{2,1,0:T(8,128)(2,1)} %stack.2), calls=%async_computation | async-start | bytes 4194304 | tf_op jit(solution)/shard_map/all_to_all | solution.py:34
  28.3 24.1 %all_gather.18 = s32[1,2048]{1,0:T(1,128)S(1)} all-gather(s32[1,128]{1,0:T(1,128)S(1)} %copy-done.6), channel_id=1, replica_groups=mesh['ctx'=16,'fsdp'=32] {'ctx'}, dimensions={1}, use_global_device_ids=true | all-gather | bytes 8704 | tf_op jit(solution)/shard_map/all_gather | solution.py:41
  53.9 211.8 %while.23 = (s32[]{:T(128)}, f32[4,4,128]{2,1,0:T(4,128)S(1)}, f32[4,4,128]{2,1,0:T(4,128)S(1)}, f32[4,4,128,128]{3,2,1,0:T(8,128)S(1)}, bf16[128,512]{0,1:T(8,1...) while((s32[]{:T(128)}, f32[4,4,128]{2,1,0:T(4,128)S(1)}, ...), condition=%wide.region_5.6_spmd, body=%wide.region_2.5_spmd.sunk | while | flops 137121808 | bytes 7801232 | solution.py:87
  53.9 2.3 collective-permute-start
  56.2 1.9 collective-permute-start.1
  58.3 8.2 %collective-permute-done = bf16[128,512]{0,1:T(8,128)(2,1)S(1)} collective-permute-done((bf16[128,512]{0,1:T(8,128)(2,1)S(1)}, bf16[128,512]{0,1:T(8,128)(2,1)S(1)}, u32[]{:S(2)}, u32[]{:S(2)}) %collective-permute-start) | collective-permute-done | bytes 131104 | tf_op jit(solution)/shard_map/while/body/eval_jaxpr/ppermute | solution.py:16
  69.1 1.9 collective-permute-start
  71.1 1.9 collective-permute-start.1
  73.2 8.1 %collective-permute-done = bf16[128,512]{0,1:T(8,128)(2,1)S(1)} collective-permute-done((bf16[128,512]{0,1:T(8,128)(2,1)S(1)}, bf16[128,512]{0,1:T(8,128)(2,1)S(1)}, u32[]{:S(2)}, u32[]{:S(2)}) %collective-permute-start) | collective-permute-done | bytes 131104 | tf_op jit(solution)/shard_map/while/body/eval_jaxpr/ppermute | solution.py:16
  81.9 2.2 collective-permute-done.1
  84.9 1.9 collective-permute-start
  86.8 1.9 collective-permute-start.1
  88.9 7.2 %collective-permute-done = bf16[128,512]{0,1:T(8,128)(2,1)S(1)} collective-permute-done((bf16[128,512]{0,1:T(8,128)(2,1)S(1)}, bf16[128,512]{0,1:T(8,128)(2,1)S(1)}, u32[]{:S(2)}, u32[]{:S(2)}) %collective-permute-start) | collective-permute-done | bytes 131104 | tf_op jit(solution)/shard_map/while/body/eval_jaxpr/ppermute | solution.py:16
  96.7 3.2 collective-permute-done.1
  100.6 1.9 collective-permute-start
  102.5 1.9 collective-permute-start.1
  104.7 6.9 %collective-permute-done = bf16[128,512]{0,1:T(8,128)(2,1)S(1)} collective-permute-done((bf16[128,512]{0,1:T(8,128)(2,1)S(1)}, bf16[128,512]{0,1:T(8,128)(2,1)S(1)}, u32[]{:S(2)}, u32[]{:S(2)}) %collective-permute-start) | collective-permute-done | bytes 131104 | tf_op jit(solution)/shard_map/while/body/eval_jaxpr/ppermute | solution.py:16
  112.2 2.5 collective-permute-done.1
  115.4 1.9 collective-permute-start
  117.3 1.9 collective-permute-start.1
  119.4 6.3 %collective-permute-done = bf16[128,512]{0,1:T(8,128)(2,1)S(1)} collective-permute-done((bf16[128,512]{0,1:T(8,128)(2,1)S(1)}, bf16[128,512]{0,1:T(8,128)(2,1)S(1)}, u32[]{:S(2)}, u32[]{:S(2)}) %collective-permute-start) | collective-permute-done | bytes 131104 | tf_op jit(solution)/shard_map/while/body/eval_jaxpr/ppermute | solution.py:16
  126.4 2.0 collective-permute-done.1
  129.1 1.9 collective-permute-start
  131.0 1.9 collective-permute-start.1
  133.1 6.6 %collective-permute-done = bf16[128,512]{0,1:T(8,128)(2,1)S(1)} collective-permute-done((bf16[128,512]{0,1:T(8,128)(2,1)S(1)}, bf16[128,512]{0,1:T(8,128)(2,1)S(1)}, u32[]{:S(2)}, u32[]{:S(2)}) %collective-permute-start) | collective-permute-done | bytes 131104 | tf_op jit(solution)/shard_map/while/body/eval_jaxpr/ppermute | solution.py:16
  142.7 1.9 collective-permute-start
  144.6 1.9 collective-permute-start.1
  146.7 6.8 %collective-permute-done = bf16[128,512]{0,1:T(8,128)(2,1)S(1)} collective-permute-done((bf16[128,512]{0,1:T(8,128)(2,1)S(1)}, bf16[128,512]{0,1:T(8,128)(2,1)S(1)}, u32[]{:S(2)}, u32[]{:S(2)}) %collective-permute-start) | collective-permute-done | bytes 131104 | tf_op jit(solution)/shard_map/while/body/eval_jaxpr/ppermute | solution.py:16
  156.7 1.9 collective-permute-start
  158.7 1.9 collective-permute-start.1
  160.8 6.3 %collective-permute-done = bf16[128,512]{0,1:T(8,128)(2,1)S(1)} collective-permute-done((bf16[128,512]{0,1:T(8,128)(2,1)S(1)}, bf16[128,512]{0,1:T(8,128)(2,1)S(1)}, u32[]{:S(2)}, u32[]{:S(2)}) %collective-permute-start) | collective-permute-done | bytes 131104 | tf_op jit(solution)/shard_map/while/body/eval_jaxpr/ppermute | solution.py:16
  169.8 1.9 collective-permute-start
  171.7 1.9 collective-permute-start.1
  173.8 5.9 %collective-permute-done = bf16[128,512]{0,1:T(8,128)(2,1)S(1)} collective-permute-done((bf16[128,512]{0,1:T(8,128)(2,1)S(1)}, bf16[128,512]{0,1:T(8,128)(2,1)S(1)}, u32[]{:S(2)}, u32[]{:S(2)}) %collective-permute-start) | collective-permute-done | bytes 131104 | tf_op jit(solution)/shard_map/while/body/eval_jaxpr/ppermute | solution.py:16
  182.3 1.9 collective-permute-start
  184.3 1.9 collective-permute-start.1
  186.4 5.8 %collective-permute-done = bf16[128,512]{0,1:T(8,128)(2,1)S(1)} collective-permute-done((bf16[128,512]{0,1:T(8,128)(2,1)S(1)}, bf16[128,512]{0,1:T(8,128)(2,1)S(1)}, u32[]{:S(2)}, u32[]{:S(2)}) %collective-permute-start) | collective-permute-done | bytes 131104 | tf_op jit(solution)/shard_map/while/body/eval_jaxpr/ppermute | solution.py:16
  194.9 1.9 collective-permute-start
  196.8 1.9 collective-permute-start.1
  198.9 7.3 %collective-permute-done = bf16[128,512]{0,1:T(8,128)(2,1)S(1)} collective-permute-done((bf16[128,512]{0,1:T(8,128)(2,1)S(1)}, bf16[128,512]{0,1:T(8,128)(2,1)S(1)}, u32[]{:S(2)}, u32[]{:S(2)}) %collective-permute-start) | collective-permute-done | bytes 131104 | tf_op jit(solution)/shard_map/while/body/eval_jaxpr/ppermute | solution.py:16
  209.3 1.9 collective-permute-start
  211.2 1.9 collective-permute-start.1
  213.3 5.9 %collective-permute-done = bf16[128,512]{0,1:T(8,128)(2,1)S(1)} collective-permute-done((bf16[128,512]{0,1:T(8,128)(2,1)S(1)}, bf16[128,512]{0,1:T(8,128)(2,1)S(1)}, u32[]{:S(2)}, u32[]{:S(2)}) %collective-permute-start) | collective-permute-done | bytes 131104 | tf_op jit(solution)/shard_map/while/body/eval_jaxpr/ppermute | solution.py:16
  219.9 2.5 collective-permute-done.1
  223.2 1.9 collective-permute-start
  225.1 1.9 collective-permute-start.1
  227.2 6.8 %collective-permute-done = bf16[128,512]{0,1:T(8,128)(2,1)S(1)} collective-permute-done((bf16[128,512]{0,1:T(8,128)(2,1)S(1)}, bf16[128,512]{0,1:T(8,128)(2,1)S(1)}, u32[]{:S(2)}, u32[]{:S(2)}) %collective-permute-start) | collective-permute-done | bytes 131104 | tf_op jit(solution)/shard_map/while/body/eval_jaxpr/ppermute | solution.py:16
  236.9 1.9 collective-permute-start
  238.8 1.9 collective-permute-start.1
  240.9 7.0 %collective-permute-done = bf16[128,512]{0,1:T(8,128)(2,1)S(1)} collective-permute-done((bf16[128,512]{0,1:T(8,128)(2,1)S(1)}, bf16[128,512]{0,1:T(8,128)(2,1)S(1)}, u32[]{:S(2)}, u32[]{:S(2)}) %collective-permute-start) | collective-permute-done | bytes 131104 | tf_op jit(solution)/shard_map/while/body/eval_jaxpr/ppermute | solution.py:16
  248.5 2.2 collective-permute-done.1
  251.4 1.9 collective-permute-start
  253.3 1.9 collective-permute-start.1
  255.5 6.8 %collective-permute-done = bf16[128,512]{0,1:T(8,128)(2,1)S(1)} collective-permute-done((bf16[128,512]{0,1:T(8,128)(2,1)S(1)}, bf16[128,512]{0,1:T(8,128)(2,1)S(1)}, u32[]{:S(2)}, u32[]{:S(2)}) %collective-permute-start) | collective-permute-done | bytes 131104 | tf_op jit(solution)/shard_map/while/body/eval_jaxpr/ppermute | solution.py:16
  262.9 2.1 collective-permute-done.1
  272.4 33.4 %all-reduce = bf16[128]{0:T(256)(128)(2,1)S(1)} all-reduce(bf16[128]{0:T(256)(128)(2,1)S(1)} %dynamic-update-slice), channel_id=1, replica_groups=mesh['ctx'=16,'fsdp'=32] {'ctx'}, use_global_device_ids=true, to_apply=%add | all-reduce | flops 128 | bytes 512
  306.0 21.6 %all_gather.19 = bf16[128,2048]{1,0:T(8,128)(2,1)S(1)} all-gather(bf16[8,2048]{1,0:T(8,128)(2,1)S(1)} %convolution_convert_fusion.1), channel_id=1, replica_groups=mesh['ctx'=16,'fsdp'=32] {'ctx'}, dimensions={0}, use_global_device_ids=true | all-gather | bytes 557056 | tf_op jit(solution)/shard_map/all_gather | solution.py:111
  327.8 24.4 %all_gather.22 = bf16[128,2048]{1,0:T(8,128)(2,1)S(1)} all-gather(bf16[8,2048]{1,0:T(8,128)(2,1)S(1)} %convolution_convert_fusion), channel_id=1, replica_groups=mesh['ctx'=16,'fsdp'=32] {'ctx'}, dimensions={0}, use_global_device_ids=true | all-gather | bytes 557056 | tf_op jit(solution)/shard_map/all_gather | solution.py:110
  352.2 3.2 fusion.55
  355.4 2.5 convolution_multiply_fusion.3
  357.9 5.5 %fusion.15 = f32[128,2048]{1,0:T(8,128)} fusion(bf16[2048,448]{1,0:T(8,128)(2,1)} %all-gather.5.cloned.1.call-done, f32[128,448]{0,1:T(8,128)S(1)} %convolution_multiply_fusion.3, bf16[128,2048]{1,0:T(8,128)(2,1)S(1)} %all_gather.22, bf16[2048,448]{1,0:T(8,128)(2,1)} %bitcast.19, f32[128,448]{0,1:T(8,128)} %fusion.55), kind=kOutput, calls=%fused_computation.27 | convolution fusion | flops 470335488 | bytes 5701632 | tf_op jit(solution)/shard_map/dot_general | solution.py:126
  363.4 3.5 fusion.9
  368.6 82.6 %reduce-scatter.2.cloned.1.call-done = bf16[8,2048]{1,0:T(8,128)(2,1)} async-done(((bf16[128,2048]{1,0:T(8,128)(2,1)}), bf16[8,2048]{1,0:T(8,128)(2,1)}) %reduce-scatter.2.cloned.1.call-update) | async-done | bytes 32784 | tf_op jit(solution)/shard_map/reduce_scatter | solution.py:129
  (219 shorter events, 47.4 us)
Async XLA Ops:
  7.2 298.6 %copy-start = (bf16[1,128,2048]{2,1,0:T(8,128)(2,1)S(1)}, bf16[1,128,2048]{2,1,0:T(8,128)(2,1)}, u32[]{:S(2)}) copy-start(bf16[1,128,2048]{2,1,0:T(8,128)(2,1)} %param.18) | copy-start | bytes 1572868
  7.2 345.1 %all-gather.5.cloned.1.call-start = ((), (), s32[]{:S(2)}) async-start(), calls=%async_computation.3 | async-start | bytes 2162688 | tf_op jit(solution)/shard_map/all_gather | solution.py:32
  10.3 17.3 %copy-start.3 = (bf16[1,128,512]{2,1,0:T(8,128)(2,1)S(1)}, bf16[1,128,512]{2,1,0:T(8,128)(2,1)}, u32[]{:S(2)}) copy-start(bf16[1,128,512]{2,1,0:T(8,128)(2,1)} %param.13) | copy-start | bytes 393220
  10.3 17.5 %copy-start.4 = (bf16[1,128,512]{2,1,0:T(8,128)(2,1)S(1)}, bf16[1,128,512]{2,1,0:T(8,128)(2,1)}, u32[]{:S(2)}) copy-start(bf16[1,128,512]{2,1,0:T(8,128)(2,1)} %param.14) | copy-start | bytes 393220
  10.3 17.6 %copy-start.2 = (bf16[1,128,2048]{2,1,0:T(8,128)(2,1)S(1)}, bf16[1,128,2048]{2,1,0:T(8,128)(2,1)}, u32[]{:S(2)}) copy-start(bf16[1,128,2048]{2,1,0:T(8,128)(2,1)} %param.12) | copy-start | bytes 1572868
  10.3 347.6 %all-to-all-start = ((bf16[32,64,448]{2,1,0:T(8,128)(2,1)}), bf16[32,64,448]{2,1,0:T(8,128)(2,1)}, u32[]{:S(2)}, u32[]{:S(2)}) async-start(bf16[32,64,448]{2,1,0:T(8,128)(2,1)} %stack.2), calls=%async_computation | async-start | bytes 4194304 | tf_op jit(solution)/shard_map/all_to_all | solution.py:34
  26.8 1.5 copy-start.6
  26.8 328.6 %all-gather.3.cloned.1.call-start = ((), (), s32[]{:S(2)}) async-start(), calls=%async_computation.2 | async-start | bytes 2162688 | tf_op jit(solution)/shard_map/all_gather | solution.py:39
  27.6 423.6 %reduce-scatter.2.cloned.1.call-start = ((), (), s32[]{:S(2)}) async-start(), calls=%async_computation.4 | async-start | bytes 557056 | tf_op jit(solution)/shard_map/reduce_scatter | solution.py:129
  53.9 12.6 %collective-permute-start = (bf16[128,512]{0,1:T(8,128)(2,1)S(1)}, bf16[128,512]{0,1:T(8,128)(2,1)S(1)}, u32[]{:S(2)}, u32[]{:S(2)}) collective-permute-start(bf16[128,512]{0,1:T(8,128)(2,1)S(1)} %get-tuple-element.383), channel_id=1, source_target_pairs={{0,32},{32,64},{64,96},{96,128},{128,160},{160,192},{192,224},{224... | collective-permute-start | bytes 393224 | tf_op jit(solution)/shard_map/while/body/eval_jaxpr/ppermute | solution.py:16
  56.2 12.2 %collective-permute-start.1 = (bf16[128,512]{0,1:T(8,128)(2,1)S(1)}, bf16[128,512]{0,1:T(8,128)(2,1)S(1)}, u32[]{:S(2)}, u32[]{:S(2)}) collective-permute-start(bf16[128,512]{0,1:T(8,128)(2,1)S(1)} %get-tuple-element.384), channel_id=1, source_target_pairs={{0,32},{32,64},{64,96},{96,128},{128,160},{160,192},{192,224},{224... | collective-permute-start | bytes 393224 | tf_op jit(solution)/shard_map/while/body/eval_jaxpr/ppermute | solution.py:16
  69.1 12.1 %collective-permute-start = (bf16[128,512]{0,1:T(8,128)(2,1)S(1)}, bf16[128,512]{0,1:T(8,128)(2,1)S(1)}, u32[]{:S(2)}, u32[]{:S(2)}) collective-permute-start(bf16[128,512]{0,1:T(8,128)(2,1)S(1)} %get-tuple-element.383), channel_id=1, source_target_pairs={{0,32},{32,64},{64,96},{96,128},{128,160},{160,192},{192,224},{224... | collective-permute-start | bytes 393224 | tf_op jit(solution)/shard_map/while/body/eval_jaxpr/ppermute | solution.py:16
  71.1 13.1 %collective-permute-start.1 = (bf16[128,512]{0,1:T(8,128)(2,1)S(1)}, bf16[128,512]{0,1:T(8,128)(2,1)S(1)}, u32[]{:S(2)}, u32[]{:S(2)}) collective-permute-start(bf16[128,512]{0,1:T(8,128)(2,1)S(1)} %get-tuple-element.384), channel_id=1, source_target_pairs={{0,32},{32,64},{64,96},{96,128},{128,160},{160,192},{192,224},{224... | collective-permute-start | bytes 393224 | tf_op jit(solution)/shard_map/while/body/eval_jaxpr/ppermute | solution.py:16
  84.9 11.2 %collective-permute-start = (bf16[128,512]{0,1:T(8,128)(2,1)S(1)}, bf16[128,512]{0,1:T(8,128)(2,1)S(1)}, u32[]{:S(2)}, u32[]{:S(2)}) collective-permute-start(bf16[128,512]{0,1:T(8,128)(2,1)S(1)} %get-tuple-element.383), channel_id=1, source_target_pairs={{0,32},{32,64},{64,96},{96,128},{128,160},{160,192},{192,224},{224... | collective-permute-start | bytes 393224 | tf_op jit(solution)/shard_map/while/body/eval_jaxpr/ppermute | solution.py:16
  86.8 13.1 %collective-permute-start.1 = (bf16[128,512]{0,1:T(8,128)(2,1)S(1)}, bf16[128,512]{0,1:T(8,128)(2,1)S(1)}, u32[]{:S(2)}, u32[]{:S(2)}) collective-permute-start(bf16[128,512]{0,1:T(8,128)(2,1)S(1)} %get-tuple-element.384), channel_id=1, source_target_pairs={{0,32},{32,64},{64,96},{96,128},{128,160},{160,192},{192,224},{224... | collective-permute-start | bytes 393224 | tf_op jit(solution)/shard_map/while/body/eval_jaxpr/ppermute | solution.py:16
  100.6 11.0 %collective-permute-start = (bf16[128,512]{0,1:T(8,128)(2,1)S(1)}, bf16[128,512]{0,1:T(8,128)(2,1)S(1)}, u32[]{:S(2)}, u32[]{:S(2)}) collective-permute-start(bf16[128,512]{0,1:T(8,128)(2,1)S(1)} %get-tuple-element.383), channel_id=1, source_target_pairs={{0,32},{32,64},{64,96},{96,128},{128,160},{160,192},{192,224},{224... | collective-permute-start | bytes 393224 | tf_op jit(solution)/shard_map/while/body/eval_jaxpr/ppermute | solution.py:16
  102.5 12.1 %collective-permute-start.1 = (bf16[128,512]{0,1:T(8,128)(2,1)S(1)}, bf16[128,512]{0,1:T(8,128)(2,1)S(1)}, u32[]{:S(2)}, u32[]{:S(2)}) collective-permute-start(bf16[128,512]{0,1:T(8,128)(2,1)S(1)} %get-tuple-element.384), channel_id=1, source_target_pairs={{0,32},{32,64},{64,96},{96,128},{128,160},{160,192},{192,224},{224... | collective-permute-start | bytes 393224 | tf_op jit(solution)/shard_map/while/body/eval_jaxpr/ppermute | solution.py:16
  115.4 10.4 %collective-permute-start = (bf16[128,512]{0,1:T(8,128)(2,1)S(1)}, bf16[128,512]{0,1:T(8,128)(2,1)S(1)}, u32[]{:S(2)}, u32[]{:S(2)}) collective-permute-start(bf16[128,512]{0,1:T(8,128)(2,1)S(1)} %get-tuple-element.383), channel_id=1, source_target_pairs={{0,32},{32,64},{64,96},{96,128},{128,160},{160,192},{192,224},{224... | collective-permute-start | bytes 393224 | tf_op jit(solution)/shard_map/while/body/eval_jaxpr/ppermute | solution.py:16
  117.3 11.0 %collective-permute-start.1 = (bf16[128,512]{0,1:T(8,128)(2,1)S(1)}, bf16[128,512]{0,1:T(8,128)(2,1)S(1)}, u32[]{:S(2)}, u32[]{:S(2)}) collective-permute-start(bf16[128,512]{0,1:T(8,128)(2,1)S(1)} %get-tuple-element.384), channel_id=1, source_target_pairs={{0,32},{32,64},{64,96},{96,128},{128,160},{160,192},{192,224},{224... | collective-permute-start | bytes 393224 | tf_op jit(solution)/shard_map/while/body/eval_jaxpr/ppermute | solution.py:16
  129.1 10.7 %collective-permute-start = (bf16[128,512]{0,1:T(8,128)(2,1)S(1)}, bf16[128,512]{0,1:T(8,128)(2,1)S(1)}, u32[]{:S(2)}, u32[]{:S(2)}) collective-permute-start(bf16[128,512]{0,1:T(8,128)(2,1)S(1)} %get-tuple-element.383), channel_id=1, source_target_pairs={{0,32},{32,64},{64,96},{96,128},{128,160},{160,192},{192,224},{224... | collective-permute-start | bytes 393224 | tf_op jit(solution)/shard_map/while/body/eval_jaxpr/ppermute | solution.py:16
  131.0 11.0 %collective-permute-start.1 = (bf16[128,512]{0,1:T(8,128)(2,1)S(1)}, bf16[128,512]{0,1:T(8,128)(2,1)S(1)}, u32[]{:S(2)}, u32[]{:S(2)}) collective-permute-start(bf16[128,512]{0,1:T(8,128)(2,1)S(1)} %get-tuple-element.384), channel_id=1, source_target_pairs={{0,32},{32,64},{64,96},{96,128},{128,160},{160,192},{192,224},{224... | collective-permute-start | bytes 393224 | tf_op jit(solution)/shard_map/while/body/eval_jaxpr/ppermute | solution.py:16
  142.7 10.8 %collective-permute-start = (bf16[128,512]{0,1:T(8,128)(2,1)S(1)}, bf16[128,512]{0,1:T(8,128)(2,1)S(1)}, u32[]{:S(2)}, u32[]{:S(2)}) collective-permute-start(bf16[128,512]{0,1:T(8,128)(2,1)S(1)} %get-tuple-element.383), channel_id=1, source_target_pairs={{0,32},{32,64},{64,96},{96,128},{128,160},{160,192},{192,224},{224... | collective-permute-start | bytes 393224 | tf_op jit(solution)/shard_map/while/body/eval_jaxpr/ppermute | solution.py:16
  144.6 11.4 %collective-permute-start.1 = (bf16[128,512]{0,1:T(8,128)(2,1)S(1)}, bf16[128,512]{0,1:T(8,128)(2,1)S(1)}, u32[]{:S(2)}, u32[]{:S(2)}) collective-permute-start(bf16[128,512]{0,1:T(8,128)(2,1)S(1)} %get-tuple-element.384), channel_id=1, source_target_pairs={{0,32},{32,64},{64,96},{96,128},{128,160},{160,192},{192,224},{224... | collective-permute-start | bytes 393224 | tf_op jit(solution)/shard_map/while/body/eval_jaxpr/ppermute | solution.py:16
  156.7 10.3 %collective-permute-start = (bf16[128,512]{0,1:T(8,128)(2,1)S(1)}, bf16[128,512]{0,1:T(8,128)(2,1)S(1)}, u32[]{:S(2)}, u32[]{:S(2)}) collective-permute-start(bf16[128,512]{0,1:T(8,128)(2,1)S(1)} %get-tuple-element.383), channel_id=1, source_target_pairs={{0,32},{32,64},{64,96},{96,128},{128,160},{160,192},{192,224},{224... | collective-permute-start | bytes 393224 | tf_op jit(solution)/shard_map/while/body/eval_jaxpr/ppermute | solution.py:16
  158.7 10.4 %collective-permute-start.1 = (bf16[128,512]{0,1:T(8,128)(2,1)S(1)}, bf16[128,512]{0,1:T(8,128)(2,1)S(1)}, u32[]{:S(2)}, u32[]{:S(2)}) collective-permute-start(bf16[128,512]{0,1:T(8,128)(2,1)S(1)} %get-tuple-element.384), channel_id=1, source_target_pairs={{0,32},{32,64},{64,96},{96,128},{128,160},{160,192},{192,224},{224... | collective-permute-start | bytes 393224 | tf_op jit(solution)/shard_map/while/body/eval_jaxpr/ppermute | solution.py:16
  169.8 10.0 %collective-permute-start = (bf16[128,512]{0,1:T(8,128)(2,1)S(1)}, bf16[128,512]{0,1:T(8,128)(2,1)S(1)}, u32[]{:S(2)}, u32[]{:S(2)}) collective-permute-start(bf16[128,512]{0,1:T(8,128)(2,1)S(1)} %get-tuple-element.383), channel_id=1, source_target_pairs={{0,32},{32,64},{64,96},{96,128},{128,160},{160,192},{192,224},{224... | collective-permute-start | bytes 393224 | tf_op jit(solution)/shard_map/while/body/eval_jaxpr/ppermute | solution.py:16
  171.7 9.9 %collective-permute-start.1 = (bf16[128,512]{0,1:T(8,128)(2,1)S(1)}, bf16[128,512]{0,1:T(8,128)(2,1)S(1)}, u32[]{:S(2)}, u32[]{:S(2)}) collective-permute-start(bf16[128,512]{0,1:T(8,128)(2,1)S(1)} %get-tuple-element.384), channel_id=1, source_target_pairs={{0,32},{32,64},{64,96},{96,128},{128,160},{160,192},{192,224},{224... | collective-permute-start | bytes 393224 | tf_op jit(solution)/shard_map/while/body/eval_jaxpr/ppermute | solution.py:16
  182.3 9.9 %collective-permute-start = (bf16[128,512]{0,1:T(8,128)(2,1)S(1)}, bf16[128,512]{0,1:T(8,128)(2,1)S(1)}, u32[]{:S(2)}, u32[]{:S(2)}) collective-permute-start(bf16[128,512]{0,1:T(8,128)(2,1)S(1)} %get-tuple-element.383), channel_id=1, source_target_pairs={{0,32},{32,64},{64,96},{96,128},{128,160},{160,192},{192,224},{224... | collective-permute-start | bytes 393224 | tf_op jit(solution)/shard_map/while/body/eval_jaxpr/ppermute | solution.py:16
  184.3 9.9 %collective-permute-start.1 = (bf16[128,512]{0,1:T(8,128)(2,1)S(1)}, bf16[128,512]{0,1:T(8,128)(2,1)S(1)}, u32[]{:S(2)}, u32[]{:S(2)}) collective-permute-start(bf16[128,512]{0,1:T(8,128)(2,1)S(1)} %get-tuple-element.384), channel_id=1, source_target_pairs={{0,32},{32,64},{64,96},{96,128},{128,160},{160,192},{192,224},{224... | collective-permute-start | bytes 393224 | tf_op jit(solution)/shard_map/while/body/eval_jaxpr/ppermute | solution.py:16
  194.9 11.3 %collective-permute-start = (bf16[128,512]{0,1:T(8,128)(2,1)S(1)}, bf16[128,512]{0,1:T(8,128)(2,1)S(1)}, u32[]{:S(2)}, u32[]{:S(2)}) collective-permute-start(bf16[128,512]{0,1:T(8,128)(2,1)S(1)} %get-tuple-element.383), channel_id=1, source_target_pairs={{0,32},{32,64},{64,96},{96,128},{128,160},{160,192},{192,224},{224... | collective-permute-start | bytes 393224 | tf_op jit(solution)/shard_map/while/body/eval_jaxpr/ppermute | solution.py:16
  196.8 11.7 %collective-permute-start.1 = (bf16[128,512]{0,1:T(8,128)(2,1)S(1)}, bf16[128,512]{0,1:T(8,128)(2,1)S(1)}, u32[]{:S(2)}, u32[]{:S(2)}) collective-permute-start(bf16[128,512]{0,1:T(8,128)(2,1)S(1)} %get-tuple-element.384), channel_id=1, source_target_pairs={{0,32},{32,64},{64,96},{96,128},{128,160},{160,192},{192,224},{224... | collective-permute-start | bytes 393224 | tf_op jit(solution)/shard_map/while/body/eval_jaxpr/ppermute | solution.py:16
  209.3 10.0 %collective-permute-start = (bf16[128,512]{0,1:T(8,128)(2,1)S(1)}, bf16[128,512]{0,1:T(8,128)(2,1)S(1)}, u32[]{:S(2)}, u32[]{:S(2)}) collective-permute-start(bf16[128,512]{0,1:T(8,128)(2,1)S(1)} %get-tuple-element.383), channel_id=1, source_target_pairs={{0,32},{32,64},{64,96},{96,128},{128,160},{160,192},{192,224},{224... | collective-permute-start | bytes 393224 | tf_op jit(solution)/shard_map/while/body/eval_jaxpr/ppermute | solution.py:16
  211.2 11.2 %collective-permute-start.1 = (bf16[128,512]{0,1:T(8,128)(2,1)S(1)}, bf16[128,512]{0,1:T(8,128)(2,1)S(1)}, u32[]{:S(2)}, u32[]{:S(2)}) collective-permute-start(bf16[128,512]{0,1:T(8,128)(2,1)S(1)} %get-tuple-element.384), channel_id=1, source_target_pairs={{0,32},{32,64},{64,96},{96,128},{128,160},{160,192},{192,224},{224... | collective-permute-start | bytes 393224 | tf_op jit(solution)/shard_map/while/body/eval_jaxpr/ppermute | solution.py:16
  223.2 10.9 %collective-permute-start = (bf16[128,512]{0,1:T(8,128)(2,1)S(1)}, bf16[128,512]{0,1:T(8,128)(2,1)S(1)}, u32[]{:S(2)}, u32[]{:S(2)}) collective-permute-start(bf16[128,512]{0,1:T(8,128)(2,1)S(1)} %get-tuple-element.383), channel_id=1, source_target_pairs={{0,32},{32,64},{64,96},{96,128},{128,160},{160,192},{192,224},{224... | collective-permute-start | bytes 393224 | tf_op jit(solution)/shard_map/while/body/eval_jaxpr/ppermute | solution.py:16
  225.1 11.0 %collective-permute-start.1 = (bf16[128,512]{0,1:T(8,128)(2,1)S(1)}, bf16[128,512]{0,1:T(8,128)(2,1)S(1)}, u32[]{:S(2)}, u32[]{:S(2)}) collective-permute-start(bf16[128,512]{0,1:T(8,128)(2,1)S(1)} %get-tuple-element.384), channel_id=1, source_target_pairs={{0,32},{32,64},{64,96},{96,128},{128,160},{160,192},{192,224},{224... | collective-permute-start | bytes 393224 | tf_op jit(solution)/shard_map/while/body/eval_jaxpr/ppermute | solution.py:16
  236.9 11.0 %collective-permute-start = (bf16[128,512]{0,1:T(8,128)(2,1)S(1)}, bf16[128,512]{0,1:T(8,128)(2,1)S(1)}, u32[]{:S(2)}, u32[]{:S(2)}) collective-permute-start(bf16[128,512]{0,1:T(8,128)(2,1)S(1)} %get-tuple-element.383), channel_id=1, source_target_pairs={{0,32},{32,64},{64,96},{96,128},{128,160},{160,192},{192,224},{224... | collective-permute-start | bytes 393224 | tf_op jit(solution)/shard_map/while/body/eval_jaxpr/ppermute | solution.py:16
  238.8 11.9 %collective-permute-start.1 = (bf16[128,512]{0,1:T(8,128)(2,1)S(1)}, bf16[128,512]{0,1:T(8,128)(2,1)S(1)}, u32[]{:S(2)}, u32[]{:S(2)}) collective-permute-start(bf16[128,512]{0,1:T(8,128)(2,1)S(1)} %get-tuple-element.384), channel_id=1, source_target_pairs={{0,32},{32,64},{64,96},{96,128},{128,160},{160,192},{192,224},{224... | collective-permute-start | bytes 393224 | tf_op jit(solution)/shard_map/while/body/eval_jaxpr/ppermute | solution.py:16
  251.4 10.9 %collective-permute-start = (bf16[128,512]{0,1:T(8,128)(2,1)S(1)}, bf16[128,512]{0,1:T(8,128)(2,1)S(1)}, u32[]{:S(2)}, u32[]{:S(2)}) collective-permute-start(bf16[128,512]{0,1:T(8,128)(2,1)S(1)} %get-tuple-element.383), channel_id=1, source_target_pairs={{0,32},{32,64},{64,96},{96,128},{128,160},{160,192},{192,224},{224... | collective-permute-start | bytes 393224 | tf_op jit(solution)/shard_map/while/body/eval_jaxpr/ppermute | solution.py:16
  253.3 11.7 %collective-permute-start.1 = (bf16[128,512]{0,1:T(8,128)(2,1)S(1)}, bf16[128,512]{0,1:T(8,128)(2,1)S(1)}, u32[]{:S(2)}, u32[]{:S(2)}) collective-permute-start(bf16[128,512]{0,1:T(8,128)(2,1)S(1)} %get-tuple-element.384), channel_id=1, source_target_pairs={{0,32},{32,64},{64,96},{96,128},{128,160},{160,192},{192,224},{224... | collective-permute-start | bytes 393224 | tf_op jit(solution)/shard_map/while/body/eval_jaxpr/ppermute | solution.py:16
  266.3 3.4 copy-start.5
  266.3 5.7 %copy-start.7 = (bf16[1,128,2]{1,2,0:T(2,128)(2,1)S(1)}, bf16[1,128,2]{1,2,0:T(2,128)(2,1)}, u32[]{:S(2)}) copy-start(bf16[1,128,2]{1,2,0:T(2,128)(2,1)} %param.17) | copy-start | bytes 1540
  357.9 5.5 %copy-start.1 = (f32[128,448]{0,1:T(8,128)S(1)}, f32[128,448]{0,1:T(8,128)}, u32[]{:S(2)}) copy-start(f32[128,448]{0,1:T(8,128)} %fusion.55) | copy-start | bytes 688132
Sparse Core Ops, SparseCore 0:
  10.1 168.0 all-gather.4
  180.3 130.6 all-gather.2
  367.1 84.0 reduce-scatter.1
